TPU v7x, 32 devices: a whole 2x2x4 slice. The times are simulated.
32 devices in a mesh: row: 8 (over z, y), col: 4 (over x, core).
Axes of the slice: x: 2, y: 2, z: 4, core: 2. Of those that a mesh axis runs over, the one named last changes fastest.
Arguments:
- points: float32 [8, 5120], P(None, ('row', 'col')), may hold values from -6 to 6
- sketch: bfloat16 [5120, 256], P(('row', 'col')), may hold values from -0.625 to 0.625
- rank: int32 [5120], P(('row', 'col')), may hold values from 0 to 5119, each once
- boundary: int32 [1], replicated, may hold values from 1280 to 3840
- scales: float32 [8], replicated, may hold values from 1.5 to 4
Outputs:
- basis: float32 [5120, 256], P(('row', 'col'))
- factor: float32 [256, 256], replicated
Inputs may be any that keep to these rules, and one draw needn't show every extreme that they name: `rank`: each tree position appears once.
All inputs are finite; a program needn't handle non-finite values.
Results may differ from a plain program's by a relative error of at most 0.0006.
The roundings to bfloat16 on the way count: a program that leaves them out, or rounds other values in their place, can miss the bound.
Values may be sent and summed in bfloat16 or wider, within the bound.
A program may use at most 64 MiB of HBM per device.

v0:
```python
import jax
import jax.numpy as jnp
from jax import lax
from jax.sharding import PartitionSpec as P


def partial_terms(tgt_pts, tgt_side, src_pts, src_side, src_tests):
    total = src_pts.shape[1]
    blocks = total // total
    ranks = src_tests.shape[1]

    def term(start, count):
        tsq = jnp.sum(tgt_pts * tgt_pts, axis=0)

        def add_block(index, acc):
            ssq = jnp.sum(src_pts * src_pts, axis=0)
            inner = lax.dot_general(
                tgt_pts,
                src_pts,
                (((0,), (0,)), ((), ())),
                precision=lax.Precision.HIGHEST,
                preferred_element_type=jnp.float32,
            )
            dist = tsq[:, None] + ssq[None, :] - 2.0 * inner
            mask = (
                tgt_side[:, None] + src_side[None, :] - 2.0 * tgt_side[:, None] * src_side[None, :]
            )
            tile = (jnp.exp(-0.5 * dist) * mask).astype(jnp.bfloat16)
            return acc + jnp.dot(tile, src_tests, preferred_element_type=jnp.float32)

        return lax.fori_loop(0, blocks, add_block, jnp.zeros((count, ranks), jnp.float32))

    return term


def body(points, sketch, rank, boundary, scales):
    scaled = points / scales[:, None]
    side = (rank >= boundary[0]).astype(jnp.float32)
    local = points.shape[1]
    ranks = sketch.shape[1]
    everyone = lax.axis_size("row") * lax.axis_size("col") * local
    tgt_pts, tgt_side = (
        lax.all_gather(scaled, "col", axis=1, tiled=True),
        lax.all_gather(side, "col", axis=0, tiled=True),
    )
    src_pts, src_side = (
        lax.all_gather(scaled, "row", axis=1, tiled=True),
        lax.all_gather(side, "row", axis=0, tiled=True),
    )
    src_tests = lax.all_gather(sketch, "row", axis=0, tiled=True)
    term = partial_terms(tgt_pts, tgt_side, src_pts, src_side, src_tests)
    sample = lax.psum_scatter(
        term(jnp.int32(0), local * lax.axis_size("col")), "col", scatter_dimension=0, tiled=True
    )
    own_gram = jnp.dot(
        sample.T, sample, precision=lax.Precision.HIGHEST, preferred_element_type=jnp.float32
    )
    gram = lax.psum(own_gram, ("row", "col")) / jnp.float32(everyone)
    shift = 0.1 * jnp.trace(gram) / jnp.float32(ranks)
    factor = jnp.linalg.cholesky(gram + shift * jnp.eye(ranks, dtype=jnp.float32))
    basis = jax.scipy.linalg.solve_triangular(factor, sample.T, lower=True).T
    return (basis, factor)


def solution(mesh):
    placed = (P(None, ("row", "col")), P(("row", "col"), None), P(("row", "col")), P(), P())
    return jax.shard_map(
        body, mesh=mesh, in_specs=placed, out_specs=(P(("row", "col"), None), P()), check_vma=False
    )
```

profile of v0, /device:TPU:0, one launch (start us, length us, event | category | flops | bytes accessed | tf_op | source)
XLA Modules:
  0.0 342.7 jit_solution(11203993560195259603)
XLA Ops:
  7.2 0.0 reduce-scatter.2.cloned.1.call-start
  7.2 0.8 divide_bitcast_fusion
  8.0 32.3 %all-gather.1 = f32[8,160,8]{1,2,0:T(8,128)S(1)} all-gather(f32[1,160,8]{1,2,0:T(8,128)S(1)} %divide_bitcast_fusion), channel_id=1, replica_groups=mesh['row'=8,'col'=4] {'row'}, dimensions={0}, use_global_device_ids=true | all-gather | bytes 46080 | tf_op jit(solution)/shard_map/all_gather | solution.py:47
  40.3 5.2 %all-gather = f32[4,160,8]{1,2,0:T(8,128)S(1)} all-gather(f32[1,160,8]{1,2,0:T(8,128)S(1)} %divide_bitcast_fusion), channel_id=1, replica_groups=mesh['row'=8,'col'=4] {'col'}, dimensions={0}, use_global_device_ids=true | all-gather | bytes 25600 | tf_op jit(solution)/shard_map/all_gather | solution.py:43
  45.5 1.2 dynamic-slice.3
  46.7 1.2 dynamic-slice.4
  49.9 0.8 fusion.14
  50.8 7.1 %all-reduce.1 = f32[640]{0:T(1024)S(1)} all-reduce(f32[640]{0:T(1024)S(1)} %get-tuple-element.67), channel_id=1, replica_groups=mesh['row'=8,'col'=4] {'col'}, use_global_device_ids=true, to_apply=%add.1 | all-reduce | flops 640 | bytes 5120
  57.9 21.7 %all-reduce.2 = f32[1280]{0:T(1024)S(1)} all-reduce(f32[1280]{0:T(1024)S(1)} %get-tuple-element.66), channel_id=1, replica_groups=mesh['row'=8,'col'=4] {'row'}, use_global_device_ids=true, to_apply=%add.2 | all-reduce | flops 1280 | bytes 10240
  79.6 0.1 reshape.58
  79.7 0.1 reshape.56
  79.8 32.1 %all_gather.19 = bf16[1280,256]{1,0:T(8,128)(2,1)S(1)} all-gather(bf16[160,256]{1,0:T(8,128)(2,1)} %param.6), channel_id=1, replica_groups=mesh['row'=8,'col'=4] {'row'}, dimensions={0}, use_global_device_ids=true | all-gather | bytes 737280 | tf_op jit(solution)/shard_map/all_gather | solution.py:50
  112.0 3.7 %fusion.4 = bf16[640,1280]{1,0:T(8,128)(2,1)S(1)} fusion(f32[640,8]{0,1:T(8,128)S(1)} %reshape.56, f32[1280,8]{0,1:T(8,128)S(1)} %reshape.58, f32[640]{0:T(1024)S(1)} %broadcast_multiply_fusion, f32[1280]{0:T(1024)S(1)} %all-reduce.2, f32[640]{0:T(1024)S(1)} %all-reduce.1, f32[1280]{0:T(1024)S(1)} %multiply_reduce_fusion, f32[640]{0:T(1024)S(1)} %multiply_reduce_fusion.1), kind=kOutput, calls=%fused_computation.7 | convolution fusion | flops 86016000 | bytes 1717760 | tf_op jit(solution)/shard_map/while/body/eval_jaxpr/dot_general | solution.py:17
  115.6 1.4 fusion.17
  117.0 0.0 reduce-scatter.2.cloned.1.call-update
  117.1 0.2 all-reduce.5.cloned.1.call-start
  117.3 18.7 %reduce-scatter.2.cloned.1.call-done = f32[160,256]{1,0:T(8,128)} async-done(((f32[640,256]{1,0:T(8,128)}), f32[160,256]{1,0:T(8,128)}) %reduce-scatter.2.cloned.1.call-update) | async-done | bytes 163856 | tf_op jit(solution)/shard_map/reduce_scatter | solution.py:52
  136.0 2.4 fusion.18
  138.3 0.0 all-reduce.5.cloned.1.call-update
  138.4 130.4 %all-reduce.5.cloned.1.call-done = f32[256,256]{0,1:T(8,128)} async-done(((f32[256,256]{0,1:T(8,128)}), f32[256,256]{0,1:T(8,128)}) %all-reduce.5.cloned.1.call-update) | async-done | bytes 262160 | tf_op jit(solution)/shard_map/psum | solution.py:58
  268.8 1.6 select_reduce_fusion
  271.0 1.0 select_add_fusion
  272.0 0.1 copy.26
  272.1 1.0 fusion.5
  273.1 11.7 %cholesky.49 = f32[128,128]{1,0:T(8,128)S(1)} custom-call(f32[128,128]{1,0:T(8,128)S(1)} %cholesky.115), custom_call_target="Cholesky" | custom-call | tf_op jit(solution)/shard_map/jit(cholesky)/cholesky | solution.py:60
  284.9 9.8 %custom-call.15 = f32[1,128,128]{1,2,0:T(8,128)S(1)} custom-call(f32[1,128,128]{2,1,0:T(8,128)S(1)} %get-tuple-element.65), custom_call_target="InvertDiagBlocksLowerTriangular" | custom-call | tf_op jit(solution)/shard_map/jit(cholesky)/cholesky | solution.py:60
  294.7 0.2 fusion.11
  294.9 0.3 convolution_subtract_fusion.1
  295.2 11.7 %cholesky.103 = f32[128,128]{1,0:T(8,128)S(1)} custom-call(f32[128,128]{1,0:T(8,128)S(1)} %convolution_subtract_fusion.1), custom_call_target="Cholesky" | custom-call | tf_op jit(solution)/shard_map/jit(cholesky)/cholesky | solution.py:60
  306.9 0.1 copy.29
  307.0 0.1 copy.28
  307.1 0.1 copy.27
  307.3 0.0 copy-start
  307.3 0.7 compare_reduce_fusion
  309.4 0.1 triangular_solve.62
  309.5 4.5 %while.1 = (s32[]{:T(128)}, f32[256,256]{0,1:T(8,128)S(1)}, s32[2,2]{1,0:T(2,128)S(1)}, f32[2,128,128]{2,1,0:T(8,128)S(1)}, s32[]{:T(128)}) while((s32[]{:T(128)}, f32[256,256]{0,1:T(8,128)S(1)}, s32[2,2]{1,0:T(2,128)S(1)}, f32[2,128,128]{2,1,0:T(8,128)S(1)}, s32[]{:T(128)}) %tuple.35), condition=%wide.while_cond, body=%wide.while_body.sunk | while | flops 2 | bytes 393321 | solution.py:61
  309.7 0.6 fusion.30
  310.3 1.4 dynamic-slice.9
  311.7 0.1 copy.35
  311.9 0.6 fusion.30
  312.5 1.4 dynamic-slice.9
  313.9 0.1 copy.35
  314.0 19.7 %custom-call.16 = f32[2,128,128]{1,2,0:T(8,128)S(1)} custom-call(f32[2,128,128]{2,1,0:T(8,128)S(1)} %get-tuple-element.33), custom_call_target="InvertDiagBlocksLowerTriangular" | custom-call | tf_op jit(solution)/shard_map/jit(_solve_triangular)/triangular_solve | solution.py:61
  333.7 0.2 fusion.7
  333.9 0.2 convolution_subtract_fusion
  334.2 0.2 fusion.10
  334.4 0.7 maximum_bitcast_fusion
  335.1 0.8 copy.31
  (21 shorter events, 0.3 us)
Async XLA Ops:
  7.2 128.8 %reduce-scatter.2.cloned.1.call-start = ((), (), s32[]{:S(2)}) async-start(), calls=%async_computation.1 | async-start | bytes 819200 | tf_op jit(solution)/shard_map/reduce_scatter | solution.py:52
  117.1 151.7 %all-reduce.5.cloned.1.call-start = ((), (), s32[]{:S(2)}) async-start(), calls=%async_computation.2 | async-start | bytes 524288 | tf_op jit(solution)/shard_map/psum | solution.py:58
  307.3 26.4 %copy-start = (f32[160,256]{1,0:T(8,128)S(1)}, f32[160,256]{1,0:T(8,128)}, u32[]{:S(2)}) copy-start(f32[160,256]{1,0:T(8,128)} %reduce-scatter.2.cloned.1.call-done) | copy-start | bytes 491524
Sparse Core Ops, SparseCore 0:
  117.2 18.7 reduce-scatter.1
  142.0 126.6 all-reduce.4
where the time goes:
time: 343 us
  waiting for transfers between devices  149 us (43%)
  blocking collectives  98.4 us (29%)
  other arithmetic  59.6 us (17%)
  between operations  18.2 us (5%)
  matrix products  8.59 us (3%)
  local copies, waits for them, and re-layouts  8.31 us (2%)
    psum x1, waiting for transfers between devices, body(): gram = lax.psum(own_gram, ('row', 'col')) / jnp.float32(everyone)  130 us
    another operation x6, other arithmetic, body(): jnp.linalg.cholesky(gram + shift * jnp.eye(ranks, dtype=jnp.float32))  34 us
    all_gather x1, blocking collectives, body(): lax.all_gather(scaled, 'row', axis=1, tiled=True)  32.3 us
    all_gather x1, blocking collectives, body(): src_tests = lax.all_gather(sketch, 'row', axis=0, tiled=True)  32.1 us
    unnamed x2, blocking collectives  28.8 us
    another operation x3, other arithmetic, body(): basis = jax.scipy.linalg.solve_triangular(factor, sample.T, lower=True).T  19.7 us
    reduce_scatter x1, waiting for transfers between devices, body(): lax.psum_scatter(term(jnp.int32(0), local * lax.axis_size('col')), 'col',...  18.7 us
  transfers between devices with their start and end apart: 2, of which 2 were waited for; matrix products, arithmetic and copies ran while one was open for 0% of the time, Pallas kernels for 0%

commit v1 on v0

v1 whole, which is shorter than its diff:
```python
import functools

import jax
import jax.numpy as jnp
from jax import lax
from jax.experimental import pallas as pl
from jax.experimental.pallas import tpu as pltpu
from jax.sharding import PartitionSpec as P

HIGHEST = lax.Precision.HIGHEST
FAR = 5000.0
VMEM = pl.BlockSpec(memory_space=pltpu.VMEM)
ANY = pl.BlockSpec(memory_space=pl.ANY)


def dot(a, b, dims, precision=HIGHEST):
    return lax.dot_general(
        a, b, (dims, ((), ())), precision=precision, preferred_element_type=jnp.float32
    )


def remote(src, dst, send, recv, row, col):
    return pltpu.make_async_remote_copy(
        src_ref=src,
        dst_ref=dst,
        send_sem=send,
        recv_sem=recv,
        device_id=(row, col),
        device_id_type=pl.DeviceIdType.MESH,
    )


def each(start, stop, step):
    def run(index, carry):
        step(index)
        return carry

    lax.fori_loop(start, stop, run, 0)


def gather_kernel(rows, cols, info, tests, srcs, tgts, bank, s_info, r_info, s_test, r_test, s_tgt, r_tgt, local):
    row, col = lax.axis_index("row"), lax.axis_index("col")
    barrier = pltpu.get_barrier_semaphore()
    each(1, rows, lambda k: pl.semaphore_signal(barrier, 1, device_id=((row + k) % rows, col), device_id_type=pl.DeviceIdType.MESH))
    each(1, cols, lambda k: pl.semaphore_signal(barrier, 1, device_id=(row, (col + k) % cols), device_id_type=pl.DeviceIdType.MESH))
    own = [
        pltpu.make_async_copy(info, srcs.at[row], local.at[0]),
        pltpu.make_async_copy(info, tgts.at[col], local.at[1]),
        pltpu.make_async_copy(tests, bank.at[row], local.at[2]),
    ]
    for copy in own:
        copy.start()
    pl.semaphore_wait(barrier, rows + cols - 2)

    def tgt(k):
        return remote(info, tgts.at[col], s_tgt.at[k], r_tgt.at[k], row, (col + k) % cols)

    def src(k):
        return remote(info, srcs.at[row], s_info.at[k], r_info.at[k], (row + k) % rows, col)

    def test(k):
        return remote(tests, bank.at[row], s_test.at[k], r_test.at[k], (row + k) % rows, col)

    each(1, cols, lambda k: tgt(k).start())
    each(1, rows, lambda k: src(k).start())
    each(1, rows, lambda k: test(k).start())
    each(1, cols, lambda k: tgt(k).wait())
    each(1, rows, lambda k: src(k).wait())
    each(1, rows, lambda k: test(k).wait())
    for copy in own:
        copy.wait()


def gather(info, tests, rows, cols):
    dma = pltpu.SemaphoreType.DMA
    return pl.pallas_call(
        functools.partial(gather_kernel, rows, cols),
        out_shape=(
            jax.ShapeDtypeStruct((rows,) + info.shape, info.dtype),
            jax.ShapeDtypeStruct((cols,) + info.shape, info.dtype),
            jax.ShapeDtypeStruct((rows,) + tests.shape, tests.dtype),
        ),
        in_specs=[ANY, ANY],
        out_specs=(ANY, ANY, ANY),
        scratch_shapes=[dma((rows,)), dma((rows,)), dma((rows,)), dma((rows,)), dma((cols,)), dma((cols,)), dma((3,))],
        compiler_params=pltpu.CompilerParams(collective_id=0, has_side_effects=True),
        name="gather",
    )(info, tests)


def tile_kernel(srcs, tgts, bank, out, left, right):
    cols, depth, local = tgts.shape
    rows = srcs.shape[0]
    for r in range(rows):
        right[:, r * local : (r + 1) * local] = srcs[r]
    sq = 8
    for place in range(cols):
        col = 2 * (place % (cols // 2)) + place // (cols // 2)
        block = tgts[col]
        half, one = block[sq : sq + 1], block[sq + 1 : sq + 2]
        side, other = block[sq + 2 : sq + 3], block[sq + 3 : sq + 4]
        left[:, place * local : (place + 1) * local] = jnp.concatenate(
            [block[:sq], one, half, -FAR * side, -FAR * other, block[sq + 4 :]], axis=0
        )
    step = 128
    source, tests = right[...], bank[...].reshape(rows * local, bank.shape[2])

    def chunk(index):
        start = pl.multiple_of(index * step, step)
        power = dot(left[:, pl.ds(start, step)].T, source, ((1,), (0,)))
        tile = jnp.exp(power).astype(jnp.bfloat16)
        out[pl.ds(start, step), :] = dot(tile, tests, ((1,), (0,)), None)

    each(0, cols * local // step, chunk)


def tiles(srcs, tgts, bank):
    rows, depth, local = srcs.shape
    cols = tgts.shape[0]
    ranks = bank.shape[2]
    return pl.pallas_call(
        tile_kernel,
        out_shape=jax.ShapeDtypeStruct((cols * local, ranks), jnp.float32),
        in_specs=[VMEM, VMEM, VMEM],
        out_specs=VMEM,
        scratch_shapes=[
            pltpu.VMEM((depth, cols * local), jnp.float32),
            pltpu.VMEM((depth, rows * local), jnp.float32),
        ],
        name="tiles",
    )(srcs, tgts, bank)


def reduce_kernel(
    rows, cols, part, sample, gram, pair, stage, far, square, mate, mine, piece, done,
    s_pair, r_pair, s_far, r_far, s_piece, r_piece, s_done, r_done,
):
    row, col = lax.axis_index("row"), lax.axis_index("col")
    half = cols // 2
    count = rows * half
    parity, spot = col % 2, col // 2
    partner = col + 1 - 2 * parity
    index = row * half + spot

    def place(i):
        return i // half, 2 * (i % half) + parity

    barrier = pltpu.get_barrier_semaphore()
    pl.semaphore_signal(barrier, 1, device_id=(row, partner), device_id_type=pl.DeviceIdType.MESH)
    each(1, count, lambda k: pl.semaphore_signal(barrier, 1, device_id=place((index + k) % count), device_id_type=pl.DeviceIdType.MESH))
    pl.semaphore_wait(barrier, count)

    swap = remote(part.at[1 - parity], pair, s_pair.at[0], r_pair.at[0], row, partner)
    swap.start()
    swap.wait()
    stage[...] = part[parity] + pair[...]

    def send(k):
        there = (spot + k) % half
        return remote(stage.at[there], far.at[k], s_far.at[k], r_far.at[k], row, 2 * there + parity)

    each(1, half, lambda k: send(k).start())
    each(1, half, lambda k: send(k).wait())
    total = stage[spot]
    for k in range(1, half):
        total = total + far[k]
    sample[...] = total

    square[...] = dot(total.T, total, ((1,), (0,))).reshape(square.shape)
    swap = remote(square.at[1 - parity], mate, s_pair.at[1], r_pair.at[1], row, partner)
    swap.start()
    swap.wait()
    mine[...] = square[parity] + mate[...]

    def scatter(k):
        there = (index + k) % count
        r, c = place(there)
        return remote(mine.at[there], piece.at[k], s_piece.at[k], r_piece.at[k], r, c)

    each(1, count, lambda k: scatter(k).start())
    each(1, count, lambda k: scatter(k).wait())
    piece[0] = mine[index]
    done[index] = jnp.sum(piece[...], axis=0)

    def collect(k):
        r, c = place((index + k) % count)
        return remote(done.at[index], done.at[index], s_done.at[k], r_done.at[k], r, c)

    each(1, count, lambda k: collect(k).start())
    each(1, count, lambda k: collect(k).wait())
    swap = remote(done, gram.at[parity], s_pair.at[2], r_pair.at[2], row, partner)
    swap.start()
    gram[parity] = done[...]
    swap.wait()


def reduce(part, rows, cols):
    local, ranks = part.shape[0] // cols, part.shape[1]
    half, count = cols // 2, rows * cols // 2
    share = ranks // 2 // count
    f32 = jnp.float32
    dma = pltpu.SemaphoreType.DMA
    sample, gram = pl.pallas_call(
        functools.partial(reduce_kernel, rows, cols),
        out_shape=(
            jax.ShapeDtypeStruct((local, ranks), f32),
            jax.ShapeDtypeStruct((2, count, share, ranks), f32),
        ),
        in_specs=[VMEM],
        out_specs=(VMEM, VMEM),
        scratch_shapes=[
            pltpu.VMEM((half, local, ranks), f32),
            pltpu.VMEM((half, local, ranks), f32),
            pltpu.VMEM((half, local, ranks), f32),
            pltpu.VMEM((2, count, share, ranks), f32),
            pltpu.VMEM((count, share, ranks), f32),
            pltpu.VMEM((count, share, ranks), f32),
            pltpu.VMEM((count, share, ranks), f32),
            pltpu.VMEM((count, share, ranks), f32),
            dma((3,)), dma((3,)), dma((half,)), dma((half,)), dma((count,)), dma((count,)), dma((count,)), dma((count,)),
        ],
        compiler_params=pltpu.CompilerParams(collective_id=1, has_side_effects=True),
        name="reduce",
    )(part.reshape(2, half, local, ranks))
    return sample, gram.reshape(ranks, ranks)


def factor_block(a):
    size, wide = a.shape[0], 8
    lane = lax.broadcasted_iota(jnp.int32, (size, size), 1)
    diag = lane == lax.broadcasted_iota(jnp.int32, (size, size), 0)
    eye = diag.astype(jnp.float32)
    both = [[a[i : i + wide], eye[i : i + wide]] for i in range(0, size, wide)]
    upper, inverse = [], []
    for b in range(size // wide):
        top, side = both[b]
        at = b * wide
        d = [[top[t : t + 1, at + u : at + u + 1] for u in range(wide)] for t in range(wide)]
        low = [[None] * wide for _ in range(wide)]
        inv = []
        for s in range(wide):
            inv.append(1.0 / d[s][s])
            for t in range(s + 1, wide):
                low[t][s] = d[s][t] * inv[s]
                for u in range(t, wide):
                    d[t][u] = d[t][u] - low[t][s] * d[s][u]
        tops, sides = [], []
        for t in range(wide):
            x, y = top[t : t + 1], side[t : t + 1]
            for s in range(t):
                x = x - low[t][s] * tops[s]
                y = y - low[t][s] * sides[s]
            tops.append(x)
            sides.append(y)
        for i in range(b + 1, size // wide):
            x, y = both[i]
            marks = []
            for t in range(wide):
                mark = both[i][0][:, at + t : at + t + 1]
                for s in range(t):
                    mark = mark - low[t][s] * marks[s]
                marks.append(mark)
            for t in range(wide):
                scaled = marks[t] * inv[t]
                x = x - scaled * tops[t]
                y = y - scaled * sides[t]
            both[i] = [x, y]
        roots = [lax.rsqrt(d[t][t]) for t in range(wide)]
        upper += [tops[t] * roots[t] for t in range(wide)]
        inverse += [sides[t] * roots[t] for t in range(wide)]
    keep = lane >= lax.broadcasted_iota(jnp.int32, (size, size), 0)
    return jnp.where(keep, jnp.concatenate(upper, axis=0), 0.0), jnp.concatenate(inverse, axis=0)


def finish_kernel(scale, gram, sample, basis, factor, up, low):
    ranks = gram.shape[0]
    half = ranks // 2
    mean = gram[...] * scale
    same = lax.broadcasted_iota(jnp.int32, (ranks, ranks), 0) == lax.broadcasted_iota(jnp.int32, (ranks, ranks), 1)
    trace = jnp.sum(jnp.sum(jnp.where(same, mean, 0.0), axis=1, keepdims=True), axis=0, keepdims=True)
    factor[...] = jnp.where(same, mean + (0.1 / ranks) * trace, mean)
    cross = factor[:half, half:]

    def one(index):
        start = pl.multiple_of(index * half, half)
        block = factor[pl.ds(start, half), pl.ds(start, half)]
        u, m = factor_block(block)
        up[index] = u
        low[index] = m

        @pl.when(index == 0)
        def _():
            lift = dot(m, cross, ((1,), (0,)))
            up[2] = lift
            factor[half:, half:] = factor[half:, half:] - dot(lift.T, lift, ((1,), (0,)))

    each(0, 2, one)
    lift = up[2]
    first = dot(sample[:, :half], low[0], ((1,), (1,)))
    second = dot(sample[:, half:] - dot(first, lift, ((1,), (0,))), low[1], ((1,), (1,)))
    basis[:, :half] = first
    basis[:, half:] = second
    factor[:half, :half] = up[0].T
    factor[:half, half:] = jnp.zeros((half, half), jnp.float32)
    factor[half:, :half] = lift.T
    factor[half:, half:] = up[1].T


def finish(gram, sample, everyone):
    ranks = gram.shape[0]
    half = ranks // 2
    return pl.pallas_call(
        functools.partial(finish_kernel, 1.0 / everyone),
        out_shape=(
            jax.ShapeDtypeStruct(sample.shape, jnp.float32),
            jax.ShapeDtypeStruct(gram.shape, jnp.float32),
        ),
        in_specs=[VMEM, VMEM],
        out_specs=(VMEM, VMEM),
        scratch_shapes=[pltpu.VMEM((3, half, half), jnp.float32), pltpu.VMEM((2, half, half), jnp.float32)],
        name="finish",
    )(gram, sample)


def body(rows, cols, points, sketch, rank, boundary, scales):
    scaled = points / scales[:, None]
    side = (rank >= boundary[0]).astype(jnp.float32)[None]
    down = -0.5 * jnp.sum(scaled * scaled, axis=0, keepdims=True)
    fill = jnp.zeros((4, points.shape[1]), jnp.float32)
    info = jnp.concatenate([scaled, down, jnp.ones_like(side), side, 1.0 - side, fill], axis=0)
    srcs, tgts, bank = gather(info, sketch, rows, cols)
    sample, gram = reduce(tiles(srcs, tgts, bank), rows, cols)
    return finish(gram, sample, rows * cols * points.shape[1])


def solution(mesh):
    placed = (P(None, ("row", "col")), P(("row", "col"), None), P(("row", "col")), P(), P())
    return jax.shard_map(
        functools.partial(body, mesh.shape["row"], mesh.shape["col"]),
        mesh=mesh,
        in_specs=placed,
        out_specs=(P(("row", "col"), None), P()),
        check_vma=False,
    )
```

time: 343 us -> 119 us (0.35)
  waiting for transfers between devices: 149 us -> 0 us
  Pallas kernels: 0 us -> 115 us
  blocking collectives: 98.4 us -> 0 us
  other arithmetic: 59.6 us -> 0.77 us
  between operations: 18.2 us -> 1.34 us
  matrix products: 8.59 us -> 0 us
  local copies, waits for them, and re-layouts: 8.31 us -> 1.88 us
    psum x1 -> x0, waiting for transfers between devices: 130 us -> none  [body(): gram = lax.psum(own_gram, ('row', 'col')) / jnp.float32(everyone)]
    pallas_call x0 -> x4, Pallas kernels: none -> 115 us  [the longest x1 56.8 us: finish(): pl.pallas_call(functools.partial(finish_kernel, 1.0 / everyone), out_shap...]
    all_gather x3 -> x0, blocking collectives: 69.7 us -> none  [the longest x1 32.3 us: body(): lax.all_gather(scaled, 'row', axis=1, tiled=True)]
    another operation x9 -> x0, other arithmetic: 53.7 us -> none  [the longest x6 34 us: body(): jnp.linalg.cholesky(gram + shift * jnp.eye(ranks, dtype=jnp.float32))]
    unnamed x2 -> x0, blocking collectives: 28.8 us -> none
    reduce_scatter x1 -> x0, waiting for transfers between devices: 18.7 us -> none  [body(): lax.psum_scatter(term(jnp.int32(0), local * lax.axis_size('col')), 'col',...]
    dot_general x3 -> x0, matrix products: 7.45 us -> none  [the longest x1 3.66 us: add_block(): lax.dot_general(tgt_pts, src_pts, (((0,), (0,)), ((), ())), precision=lax...]
    another operation x18 -> x1, local copies, waits for them, and re-layouts: 4.65 us -> 0.01 us
  transfers between devices with their start and end apart: 2 -> 0, of which waited for: 2 -> 0; matrix products, arithmetic and copies ran while one was open for 0% -> 0% of each run, Pallas kernels for 0% -> 0%
where the time goes in v1:
time: 119 us
  Pallas kernels  115 us (97%)
  local copies, waits for them, and re-layouts  1.88 us (2%)
  between operations  1.34 us (1%)
    pallas_call x1, Pallas kernels, finish(): pl.pallas_call(functools.partial(finish_kernel, 1.0 / everyone), out_shap...  56.8 us
    pallas_call x1, Pallas kernels, reduce(): pl.pallas_call(functools.partial(reduce_kernel, rows, cols), out_shape=(j...  30.7 us
    pallas_call x1, Pallas kernels, gather(): pl.pallas_call(functools.partial(gather_kernel, rows, cols), out_shape=(j...  20.6 us
    pallas_call x1, Pallas kernels, tiles(): pl.pallas_call(tile_kernel, out_shape=jax.ShapeDtypeStruct((cols * local,...  6.77 us

profile of v1, /device:TPU:0, one launch (start us, length us, event | category | flops | bytes accessed | tf_op | source)
XLA Modules:
  0.0 118.8 jit_solution(14903279480603327089)
XLA Ops:
  0.6 0.0 copy-start
  1.3 0.7 broadcast_subtract_fusion
  2.0 0.0 copy-start.1
  2.0 0.0 copy-done
  2.0 0.7 copy-done.1
  2.6 0.1 multiply_reduce_fusion
  2.8 1.2 %concatenate.3.info = f32[16,160]{1,0:T(8,128)} concatenate(f32[8,160]{1,0:T(8,128)S(1)} %get-tuple-element.15, f32[1,160]{1,0:T(1,128)S(1)} %bitcast.11, f32[1,160]{1,0:T(1,128)S(1)} %broadcast.17, f32[1,160]{1,0:T(1,128)S(1)} %bitcast.10, f32[1,160]{1,0:T(1,128)S(1)} %bitcast.9, f32[4,160]{1,0:T(4,128)S(1)} %broadcast_in_dim.9), dimensions={0} | concatenate | bytes 20480 | tf_op jit(solution)/shard_map/concatenate | solution.py:330
  4.0 20.6 %gather.1 = (f32[8,16,160]{2,1,0:T(8,128)}, f32[4,16,160]{2,1,0:T(8,128)}, bf16[8,160,256]{2,1,0:T(8,128)(2,1)}) custom-call(f32[16,160]{1,0:T(8,128)} %concatenate.3.info, bf16[160,256]{1,0:T(8,128)(2,1)} %tests.1), custom_call_target="tpu_custom_call" | custom-call | tf_op jit(solution)/shard_map/gather/pallas_call | solution.py:76
  24.6 6.8 %tiles.1 = f32[640,256]{1,0:T(8,128)} custom-call(f32[8,16,160]{2,1,0:T(8,128)} %get-tuple-element.7.srcs, f32[4,16,160]{2,1,0:T(8,128)} %get-tuple-element.8.tgts, bf16[8,160,256]{2,1,0:T(8,128)(2,1)} %get-tuple-element.9.bank), custom_call_target="tpu_custom_call" | custom-call | tf_op jit(solution)/shard_map/tiles/pallas_call | solution.py:121
  31.3 30.7 %reduce.1 = (f32[160,256]{1,0:T(8,128)}, f32[2,16,8,256]{3,2,1,0:T(8,128)}) custom-call(f32[2,2,160,256]{3,2,1,0:T(8,128)} %bitcast.7), custom_call_target="tpu_custom_call" | custom-call | tf_op jit(solution)/shard_map/reduce/pallas_call | solution.py:203
  62.0 56.8 %finish.1 = (f32[160,256]{1,0:T(8,128)}, f32[256,256]{1,0:T(8,128)}) custom-call(f32[256,256]{1,0:T(8,128)} %bitcast.8, f32[160,256]{1,0:T(8,128)} %get-tuple-element.11.sample), custom_call_target="tpu_custom_call" | custom-call | tf_op jit(solution)/shard_map/finish/pallas_call | solution.py:312
  (3 shorter events, 0.0 us)
Async XLA Ops:
  0.6 1.4 %copy-start = (f32[8,160]{1,0:T(8,128)S(1)}, f32[8,160]{1,0:T(8,128)}, u32[]{:S(2)}) copy-start(f32[8,160]{1,0:T(8,128)} %param.5) | copy-start | bytes 15364
  2.0 0.7 copy-start.1

commit v2 on v1

--- a/solution.py
+++ b/solution.py
@@ -227,49 +227,47 @@
 
 def factor_block(a):
     size, wide = a.shape[0], 8
-    lane = lax.broadcasted_iota(jnp.int32, (size, size), 1)
-    diag = lane == lax.broadcasted_iota(jnp.int32, (size, size), 0)
-    eye = diag.astype(jnp.float32)
-    both = [[a[i : i + wide], eye[i : i + wide]] for i in range(0, size, wide)]
+    shape = (wide, size)
+    lane = lax.broadcasted_iota(jnp.int32, shape, 1)
+    line = lax.broadcasted_iota(jnp.int32, shape, 0)
+
+    def spread(x):
+        return jnp.broadcast_to(x, shape)
+
+    blocks = [a[i : i + wide] for i in range(0, size, wide)]
     upper, inverse = [], []
     for b in range(size // wide):
-        top, side = both[b]
         at = b * wide
-        d = [[top[t : t + 1, at + u : at + u + 1] for u in range(wide)] for t in range(wide)]
-        low = [[None] * wide for _ in range(wide)]
-        inv = []
+        inside = (lane >= at) & (lane < at + wide)
+        x = blocks[b]
+        y = jnp.where(inside, jnp.where(lane - at == line, 1.0, 0.0), x)
+        marks = [spread(x[:, at + u : at + u + 1]) for u in range(wide)]
+        over, root = jnp.zeros(shape, jnp.float32), jnp.zeros(shape, jnp.float32)
         for s in range(wide):
-            inv.append(1.0 / d[s][s])
-            for t in range(s + 1, wide):
-                low[t][s] = d[s][t] * inv[s]
-                for u in range(t, wide):
-                    d[t][u] = d[t][u] - low[t][s] * d[s][u]
-        tops, sides = [], []
-        for t in range(wide):
-            x, y = top[t : t + 1], side[t : t + 1]
-            for s in range(t):
-                x = x - low[t][s] * tops[s]
-                y = y - low[t][s] * sides[s]
-            tops.append(x)
-            sides.append(y)
+            pivot = spread(marks[s][s : s + 1])
+            inv = 1.0 / pivot
+            over = jnp.where(line == s, inv, over)
+            root = jnp.where(line == s, pivot, root)
+            if s + 1 < wide:
+                low = jnp.where(line > s, marks[s] * inv, 0.0)
+                for u in range(s + 1, wide):
+                    marks[u] = marks[u] - low * spread(marks[u][s : s + 1])
+                x = x - low * spread(x[s : s + 1])
+                y = y - low * spread(y[s : s + 1])
+        z = y * over
+        for s in range(wide - 1, 0, -1):
+            z = z - jnp.where(line < s, marks[s] * over, 0.0) * spread(z[s : s + 1])
+        rows = [spread(z[t : t + 1]) for t in range(wide)]
         for i in range(b + 1, size // wide):
-            x, y = both[i]
-            marks = []
-            for t in range(wide):
-                mark = both[i][0][:, at + t : at + t + 1]
-                for s in range(t):
-                    mark = mark - low[t][s] * marks[s]
-                marks.append(mark)
-            for t in range(wide):
-                scaled = marks[t] * inv[t]
-                x = x - scaled * tops[t]
-                y = y - scaled * sides[t]
-            both[i] = [x, y]
-        roots = [lax.rsqrt(d[t][t]) for t in range(wide)]
-        upper += [tops[t] * roots[t] for t in range(wide)]
-        inverse += [sides[t] * roots[t] for t in range(wide)]
-    keep = lane >= lax.broadcasted_iota(jnp.int32, (size, size), 0)
-    return jnp.where(keep, jnp.concatenate(upper, axis=0), 0.0), jnp.concatenate(inverse, axis=0)
+            old = blocks[i]
+            parts = [spread(old[:, at + t : at + t + 1]) * rows[t] for t in range(wide)]
+            while len(parts) > 1:
+                parts = [p + q for p, q in zip(parts[::2], parts[1::2])]
+            blocks[i] = jnp.where(inside, 0.0, old) - parts[0]
+        root = lax.rsqrt(root)
+        upper.append(jnp.where(lane >= at + line, x * root, 0.0))
+        inverse.append(jnp.where(lane <= at + line, y * root, 0.0))
+    return jnp.concatenate(upper, axis=0), jnp.concatenate(inverse, axis=0)
 
 
 def finish_kernel(scale, gram, sample, basis, factor, up, low):

time: 119 us -> 76 us (0.64)
  Pallas kernels: 115 us -> 71.8 us
    pallas_call x1, Pallas kernels: 56.8 us -> 13.8 us  [finish(): pl.pallas_call(functools.partial(finish_kernel, 1.0 / everyone), out_shap...]
where the time goes in v2:
time: 76 us; the launch traced here: 75.8 us
  Pallas kernels  71.8 us (94%)
  local copies, waits for them, and re-layouts  1.88 us (2%)
  between operations  1.34 us (2%)
  other arithmetic  0.77 us (1%)
    pallas_call x1, Pallas kernels, reduce(): pl.pallas_call(functools.partial(reduce_kernel, rows, cols), out_shape=(j...  30.7 us
    pallas_call x1, Pallas kernels, gather(): pl.pallas_call(functools.partial(gather_kernel, rows, cols), out_shape=(j...  20.6 us
    pallas_call x1, Pallas kernels, finish(): pl.pallas_call(functools.partial(finish_kernel, 1.0 / everyone), out_shap...  13.8 us
    pallas_call x1, Pallas kernels, tiles(): pl.pallas_call(tile_kernel, out_shape=jax.ShapeDtypeStruct((cols * local,...  6.77 us

profile of v2, /device:TPU:0, one launch (start us, length us, event | category | flops | bytes accessed | tf_op | source)
XLA Modules:
  0.0 75.8 jit_solution(959899893510936965)
XLA Ops:
  0.6 0.0 copy-start
  1.3 0.7 broadcast_subtract_fusion
  2.0 0.0 copy-start.1
  2.0 0.0 copy-done
  2.0 0.7 copy-done.1
  2.6 0.1 multiply_reduce_fusion
  2.8 1.2 %concatenate.3.info = f32[16,160]{1,0:T(8,128)} concatenate(f32[8,160]{1,0:T(8,128)S(1)} %get-tuple-element.15, f32[1,160]{1,0:T(1,128)S(1)} %bitcast.11, f32[1,160]{1,0:T(1,128)S(1)} %broadcast.17, f32[1,160]{1,0:T(1,128)S(1)} %bitcast.10, f32[1,160]{1,0:T(1,128)S(1)} %bitcast.9, f32[4,160]{1,0:T(4,128)S(1)} %broadcast_in_dim.9), dimensions={0} | concatenate | bytes 20480 | tf_op jit(solution)/shard_map/concatenate | solution.py:328
  4.0 20.6 %gather.1 = (f32[8,16,160]{2,1,0:T(8,128)}, f32[4,16,160]{2,1,0:T(8,128)}, bf16[8,160,256]{2,1,0:T(8,128)(2,1)}) custom-call(f32[16,160]{1,0:T(8,128)} %concatenate.3.info, bf16[160,256]{1,0:T(8,128)(2,1)} %tests.1), custom_call_target="tpu_custom_call" | custom-call | tf_op jit(solution)/shard_map/gather/pallas_call | solution.py:76
  24.6 6.8 %tiles.1 = f32[640,256]{1,0:T(8,128)} custom-call(f32[8,16,160]{2,1,0:T(8,128)} %get-tuple-element.7.srcs, f32[4,16,160]{2,1,0:T(8,128)} %get-tuple-element.8.tgts, bf16[8,160,256]{2,1,0:T(8,128)(2,1)} %get-tuple-element.9.bank), custom_call_target="tpu_custom_call" | custom-call | tf_op jit(solution)/shard_map/tiles/pallas_call | solution.py:121
  31.3 30.7 %reduce.1 = (f32[160,256]{1,0:T(8,128)}, f32[2,16,8,256]{3,2,1,0:T(8,128)}) custom-call(f32[2,2,160,256]{3,2,1,0:T(8,128)} %bitcast.7), custom_call_target="tpu_custom_call" | custom-call | tf_op jit(solution)/shard_map/reduce/pallas_call | solution.py:203
  62.0 13.8 %finish.1 = (f32[160,256]{1,0:T(8,128)}, f32[256,256]{1,0:T(8,128)}) custom-call(f32[256,256]{1,0:T(8,128)} %bitcast.8, f32[160,256]{1,0:T(8,128)} %get-tuple-element.11.sample), custom_call_target="tpu_custom_call" | custom-call | tf_op jit(solution)/shard_map/finish/pallas_call | solution.py:310
  (3 shorter events, 0.0 us)
Async XLA Ops:
  0.6 1.4 %copy-start = (f32[8,160]{1,0:T(8,128)S(1)}, f32[8,160]{1,0:T(8,128)}, u32[]{:S(2)}) copy-start(f32[8,160]{1,0:T(8,128)} %param.5) | copy-start | bytes 15364
  2.0 0.7 copy-start.1

commit v3 on v2

--- a/solution.py
+++ b/solution.py
@@ -10,7 +10,6 @@
 HIGHEST = lax.Precision.HIGHEST
 FAR = 5000.0
 VMEM = pl.BlockSpec(memory_space=pltpu.VMEM)
-ANY = pl.BlockSpec(memory_space=pl.ANY)
 
 
 def dot(a, b, dims, precision=HIGHEST):
@@ -38,102 +37,135 @@
     lax.fori_loop(start, stop, run, 0)
 
 
-def gather_kernel(rows, cols, info, tests, srcs, tgts, bank, s_info, r_info, s_test, r_test, s_tgt, r_tgt, local):
+def tile_kernel(
+    rows, cols, info, tests, out, srcs, tgts, bank, left,
+    s_tgt, r_tgt, s_along, r_along, s_info, r_info, s_over, r_over, s_mate, r_mate,
+):
     row, col = lax.axis_index("row"), lax.axis_index("col")
+    lines = rows // 2
+    line, odd = row // 2, row % 2
+    mate = row + 1 - 2 * odd
+    local = tests.shape[0]
+
+    def at(k):
+        return 2 * ((line + k) % lines) + odd
+
+    def origin(k):
+        return 2 * ((line + lines - k) % lines) + odd
+
     barrier = pltpu.get_barrier_semaphore()
-    each(1, rows, lambda k: pl.semaphore_signal(barrier, 1, device_id=((row + k) % rows, col), device_id_type=pl.DeviceIdType.MESH))
-    each(1, cols, lambda k: pl.semaphore_signal(barrier, 1, device_id=(row, (col + k) % cols), device_id_type=pl.DeviceIdType.MESH))
-    own = [
-        pltpu.make_async_copy(info, srcs.at[row], local.at[0]),
-        pltpu.make_async_copy(info, tgts.at[col], local.at[1]),
-        pltpu.make_async_copy(tests, bank.at[row], local.at[2]),
-    ]
-    for copy in own:
-        copy.start()
-    pl.semaphore_wait(barrier, rows + cols - 2)
+    mesh = pl.DeviceIdType.MESH
+    each(1, cols, lambda k: pl.semaphore_signal(barrier, 1, device_id=(row, (col + k) % cols), device_id_type=mesh))
+    each(1, lines, lambda k: pl.semaphore_signal(barrier, 1, device_id=(at(k), col), device_id_type=mesh))
+    pl.semaphore_signal(barrier, 1, device_id=(mate, col), device_id_type=mesh)
+    srcs[row] = info[...]
+    tgts[col] = info[...]
+    bank[row] = tests[...]
+    pl.semaphore_wait(barrier, cols + lines - 1)
 
     def tgt(k):
         return remote(info, tgts.at[col], s_tgt.at[k], r_tgt.at[k], row, (col + k) % cols)
 
-    def src(k):
-        return remote(info, srcs.at[row], s_info.at[k], r_info.at[k], (row + k) % rows, col)
-
-    def test(k):
-        return remote(tests, bank.at[row], s_test.at[k], r_test.at[k], (row + k) % rows, col)
+    def along(k):
+        return (
+            remote(info, srcs.at[row], s_info.at[k], r_info.at[k], at(k), col),
+            remote(tests, bank.at[row], s_along.at[k], r_along.at[k], at(k), col),
+        )
+
+    def over(k):
+        place = origin(k)
+        return (
+            remote(srcs.at[place], srcs.at[place], s_mate.at[k], r_mate.at[k], mate, col),
+            remote(bank.at[place], bank.at[place], s_over.at[k], r_over.at[k], mate, col),
+        )
+
+    def first():
+        return (
+            remote(info, srcs.at[row], s_mate.at[0], r_mate.at[0], mate, col),
+            remote(tests, bank.at[row], s_over.at[0], r_over.at[0], mate, col),
+        )
+
+    def go(copies):
+        for copy in copies:
+            copy.start()
+
+    def come(copies):
+        for copy in copies:
+            copy.wait_recv()
+
+    def leave(copies):
+        for copy in copies:
+            copy.wait_send()
 
     each(1, cols, lambda k: tgt(k).start())
-    each(1, rows, lambda k: src(k).start())
-    each(1, rows, lambda k: test(k).start())
+    go(first())
+    each(1, lines, lambda k: go(along(k)))
     each(1, cols, lambda k: tgt(k).wait())
-    each(1, rows, lambda k: src(k).wait())
-    each(1, rows, lambda k: test(k).wait())
-    for copy in own:
-        copy.wait()
-
-
-def gather(info, tests, rows, cols):
+    sq = 8
+    for place in range(cols):
+        block = tgts[2 * (place % (cols // 2)) + place // (cols // 2)]
+        half, one = block[sq : sq + 1], block[sq + 1 : sq + 2]
+        side, other = block[sq + 2 : sq + 3], block[sq + 3 : sq + 4]
+        left[place * local : (place + 1) * local, :] = jnp.concatenate(
+            [block[:sq], one, half, -FAR * side, -FAR * other, block[sq + 4 :]], axis=0
+        ).T
+    step = 2 * local
+
+    def add(place, fresh=False):
+        source, test = srcs[place], bank[place]
+
+        def chunk(index):
+            rows_of = pl.ds(pl.multiple_of(index * step, step), step)
+            power = dot(left[rows_of, :], source, ((1,), (0,)))
+            tile = jnp.exp(power).astype(jnp.bfloat16)
+            term = dot(tile, test, ((1,), (0,)), None)
+            out[rows_of, :] = term if fresh else out[rows_of, :] + term
+
+        each(0, cols // 2, chunk)
+
+    add(row, True)
+
+    def turn(k):
+        come(along(k))
+        go(over(k))
+        add(origin(k))
+        come(over(k - 1))
+        add(origin(k - 1) + 1 - 2 * odd)
+
+    each(1, lines, turn)
+    come(over(lines - 1))
+    add(origin(lines - 1) + 1 - 2 * odd)
+    leave(first())
+    each(1, lines, lambda k: leave(along(k) + over(k)))
+
+
+def tiles(info, tests, rows, cols):
+    depth, local = info.shape
+    ranks = tests.shape[1]
+    lines = rows // 2
     dma = pltpu.SemaphoreType.DMA
     return pl.pallas_call(
-        functools.partial(gather_kernel, rows, cols),
-        out_shape=(
-            jax.ShapeDtypeStruct((rows,) + info.shape, info.dtype),
-            jax.ShapeDtypeStruct((cols,) + info.shape, info.dtype),
-            jax.ShapeDtypeStruct((rows,) + tests.shape, tests.dtype),
-        ),
-        in_specs=[ANY, ANY],
-        out_specs=(ANY, ANY, ANY),
-        scratch_shapes=[dma((rows,)), dma((rows,)), dma((rows,)), dma((rows,)), dma((cols,)), dma((cols,)), dma((3,))],
-        compiler_params=pltpu.CompilerParams(collective_id=0, has_side_effects=True),
-        name="gather",
-    )(info, tests)
-
-
-def tile_kernel(srcs, tgts, bank, out, left, right):
-    cols, depth, local = tgts.shape
-    rows = srcs.shape[0]
-    for r in range(rows):
-        right[:, r * local : (r + 1) * local] = srcs[r]
-    sq = 8
-    for place in range(cols):
-        col = 2 * (place % (cols // 2)) + place // (cols // 2)
-        block = tgts[col]
-        half, one = block[sq : sq + 1], block[sq + 1 : sq + 2]
-        side, other = block[sq + 2 : sq + 3], block[sq + 3 : sq + 4]
-        left[:, place * local : (place + 1) * local] = jnp.concatenate(
-            [block[:sq], one, half, -FAR * side, -FAR * other, block[sq + 4 :]], axis=0
-        )
-    step = 128
-    source, tests = right[...], bank[...].reshape(rows * local, bank.shape[2])
-
-    def chunk(index):
-        start = pl.multiple_of(index * step, step)
-        power = dot(left[:, pl.ds(start, step)].T, source, ((1,), (0,)))
-        tile = jnp.exp(power).astype(jnp.bfloat16)
-        out[pl.ds(start, step), :] = dot(tile, tests, ((1,), (0,)), None)
-
-    each(0, cols * local // step, chunk)
-
-
-def tiles(srcs, tgts, bank):
-    rows, depth, local = srcs.shape
-    cols = tgts.shape[0]
-    ranks = bank.shape[2]
-    return pl.pallas_call(
-        tile_kernel,
+        functools.partial(tile_kernel, rows, cols),
         out_shape=jax.ShapeDtypeStruct((cols * local, ranks), jnp.float32),
-        in_specs=[VMEM, VMEM, VMEM],
+        in_specs=[VMEM, VMEM],
         out_specs=VMEM,
         scratch_shapes=[
-            pltpu.VMEM((depth, cols * local), jnp.float32),
-            pltpu.VMEM((depth, rows * local), jnp.float32),
+            pltpu.VMEM((rows, depth, local), jnp.float32),
+            pltpu.VMEM((cols, depth, local), jnp.float32),
+            pltpu.VMEM((rows, local, ranks), tests.dtype),
+            pltpu.VMEM((cols * local, depth), jnp.float32),
+            dma((cols,)), dma((cols,)),
+            dma((lines,)), dma((lines,)), dma((lines,)), dma((lines,)),
+            dma((lines,)), dma((lines,)), dma((lines,)), dma((lines,)),
         ],
+        compiler_params=pltpu.CompilerParams(collective_id=0, has_side_effects=True),
         name="tiles",
-    )(srcs, tgts, bank)
+    )(info, tests)
 
 
 def reduce_kernel(
     rows, cols, part, sample, gram, pair, stage, far, square, mate, mine, piece, done,
-    s_pair, r_pair, s_far, r_far, s_piece, r_piece, s_done, r_done,
+    s_pair, r_pair, s_far, r_far, s_mate, r_mate, s_piece, r_piece, s_done, r_done, s_over, r_over,
 ):
     row, col = lax.axis_index("row"), lax.axis_index("col")
     half = cols // 2
@@ -150,16 +182,27 @@
     each(1, count, lambda k: pl.semaphore_signal(barrier, 1, device_id=place((index + k) % count), device_id_type=pl.DeviceIdType.MESH))
     pl.semaphore_wait(barrier, count)
 
-    swap = remote(part.at[1 - parity], pair, s_pair.at[0], r_pair.at[0], row, partner)
-    swap.start()
-    swap.wait()
-    stage[...] = part[parity] + pair[...]
+    def swap(k):
+        there = (spot + k) % half
+        return remote(part.at[1 - parity, there], pair.at[there], s_pair.at[k], r_pair.at[k], row, partner)
 
     def send(k):
         there = (spot + k) % half
         return remote(stage.at[there], far.at[k], s_far.at[k], r_far.at[k], row, 2 * there + parity)
 
-    each(1, half, lambda k: send(k).start())
+    def merge(k):
+        there = (spot + k) % half
+        swap(k).wait()
+        stage[there] = part[parity, there] + pair[there]
+
+    def forward(k):
+        merge(k)
+        send(k).start()
+
+    each(1, half, lambda k: swap(k).start())
+    swap(0).start()
+    each(1, half, forward)
+    merge(0)
     each(1, half, lambda k: send(k).wait())
     total = stage[spot]
     for k in range(1, half):
@@ -167,9 +210,9 @@
     sample[...] = total
 
     square[...] = dot(total.T, total, ((1,), (0,))).reshape(square.shape)
-    swap = remote(square.at[1 - parity], mate, s_pair.at[1], r_pair.at[1], row, partner)
-    swap.start()
-    swap.wait()
+    trade = remote(square.at[1 - parity], mate, s_mate.at[0], r_mate.at[0], row, partner)
+    trade.start()
+    trade.wait()
     mine[...] = square[parity] + mate[...]
 
     def scatter(k):
@@ -180,18 +223,28 @@
     each(1, count, lambda k: scatter(k).start())
     each(1, count, lambda k: scatter(k).wait())
     piece[0] = mine[index]
-    done[index] = jnp.sum(piece[...], axis=0)
+    done[...] = jnp.sum(piece[...], axis=0)
+    gram[parity, index] = done[...]
 
     def collect(k):
         r, c = place((index + k) % count)
-        return remote(done.at[index], done.at[index], s_done.at[k], r_done.at[k], r, c)
-
+        return remote(done, gram.at[parity, index], s_done.at[k], r_done.at[k], r, c)
+
+    def pass_on(k):
+        there = (index + count - k) % count
+        return remote(gram.at[parity, there], gram.at[parity, there], s_over.at[k], r_over.at[k], row, partner)
+
+    def relay(k):
+        collect(k).wait_recv()
+        pass_on(k).start()
+
+    own = remote(done, gram.at[parity, index], s_over.at[0], r_over.at[0], row, partner)
     each(1, count, lambda k: collect(k).start())
-    each(1, count, lambda k: collect(k).wait())
-    swap = remote(done, gram.at[parity], s_pair.at[2], r_pair.at[2], row, partner)
-    swap.start()
-    gram[parity] = done[...]
-    swap.wait()
+    own.start()
+    each(1, count, relay)
+    own.wait()
+    each(1, count, lambda k: pass_on(k).wait())
+    each(1, count, lambda k: collect(k).wait_send())
 
 
 def reduce(part, rows, cols):
@@ -216,8 +269,8 @@
             pltpu.VMEM((count, share, ranks), f32),
             pltpu.VMEM((count, share, ranks), f32),
             pltpu.VMEM((count, share, ranks), f32),
-            pltpu.VMEM((count, share, ranks), f32),
-            dma((3,)), dma((3,)), dma((half,)), dma((half,)), dma((count,)), dma((count,)), dma((count,)), dma((count,)),
+            pltpu.VMEM((share, ranks), f32),
+            dma((half,)), dma((half,)), dma((half,)), dma((half,)), dma((1,)), dma((1,)), dma((count,)), dma((count,)), dma((count,)), dma((count,)), dma((count,)), dma((count,)),
         ],
         compiler_params=pltpu.CompilerParams(collective_id=1, has_side_effects=True),
         name="reduce",
@@ -326,8 +379,7 @@
     down = -0.5 * jnp.sum(scaled * scaled, axis=0, keepdims=True)
     fill = jnp.zeros((4, points.shape[1]), jnp.float32)
     info = jnp.concatenate([scaled, down, jnp.ones_like(side), side, 1.0 - side, fill], axis=0)
-    srcs, tgts, bank = gather(info, sketch, rows, cols)
-    sample, gram = reduce(tiles(srcs, tgts, bank), rows, cols)
+    sample, gram = reduce(tiles(info, sketch, rows, cols), rows, cols)
     return finish(gram, sample, rows * cols * points.shape[1])
 
 

time: 76 us -> 69.1 us (0.909)
  Pallas kernels: 71.8 us -> 64.8 us
    pallas_call x2 -> x1, Pallas kernels: 27.3 us -> 23.2 us  [tiles(): pl.pallas_call(functools.partial(tile_kernel, rows, cols), out_shape=jax....]
    pallas_call x1, Pallas kernels: 30.7 us -> 27.9 us  [reduce(): pl.pallas_call(functools.partial(reduce_kernel, rows, cols), out_shape=(j...]
where the time goes in v3:
time: 69.1 us; the launch traced here: 68.8 us
  Pallas kernels  64.8 us (94%)
  local copies, waits for them, and re-layouts  1.88 us (3%)
  between operations  1.34 us (2%)
  other arithmetic  0.77 us (1%)
    pallas_call x1, Pallas kernels, reduce(): pl.pallas_call(functools.partial(reduce_kernel, rows, cols), out_shape=(j...  27.9 us
    pallas_call x1, Pallas kernels, tiles(): pl.pallas_call(functools.partial(tile_kernel, rows, cols), out_shape=jax....  23.2 us
    pallas_call x1, Pallas kernels, finish(): pl.pallas_call(functools.partial(finish_kernel, 1.0 / everyone), out_shap...  13.8 us

profile of v3, /device:TPU:0, one launch (start us, length us, event | category | flops | bytes accessed | tf_op | source)
XLA Modules:
  0.0 68.8 jit_solution(752842364368085000)
XLA Ops:
  0.6 0.0 copy-start
  1.3 0.7 broadcast_subtract_fusion
  2.0 0.0 copy-start.1
  2.0 0.0 copy-done
  2.0 0.7 copy-done.1
  2.6 0.1 multiply_reduce_fusion
  2.8 1.2 %concatenate.3.info = f32[16,160]{1,0:T(8,128)} concatenate(f32[8,160]{1,0:T(8,128)S(1)} %get-tuple-element.9, f32[1,160]{1,0:T(1,128)S(1)} %bitcast.11, f32[1,160]{1,0:T(1,128)S(1)} %broadcast.17, f32[1,160]{1,0:T(1,128)S(1)} %bitcast.10, f32[1,160]{1,0:T(1,128)S(1)} %bitcast.9, f32[4,160]{1,0:T(4,128)S(1)} %broadcast_in_dim.9), dimensions={0} | concatenate | bytes 20480 | tf_op jit(solution)/shard_map/concatenate | solution.py:381
  4.0 23.2 %tiles.1 = f32[640,256]{1,0:T(8,128)} custom-call(f32[16,160]{1,0:T(8,128)} %concatenate.3.info, bf16[160,256]{1,0:T(8,128)(2,1)} %tests.1), custom_call_target="tpu_custom_call" | custom-call | tf_op jit(solution)/shard_map/tiles/pallas_call | solution.py:147
  27.2 27.9 %reduce.1 = (f32[160,256]{1,0:T(8,128)}, f32[2,16,8,256]{3,2,1,0:T(8,128)}) custom-call(f32[2,2,160,256]{3,2,1,0:T(8,128)} %bitcast.7), custom_call_target="tpu_custom_call" | custom-call | tf_op jit(solution)/shard_map/reduce/pallas_call | solution.py:256
  55.0 13.8 %finish.1 = (f32[160,256]{1,0:T(8,128)}, f32[256,256]{1,0:T(8,128)}) custom-call(f32[256,256]{1,0:T(8,128)} %bitcast.8, f32[160,256]{1,0:T(8,128)} %get-tuple-element.5.sample), custom_call_target="tpu_custom_call" | custom-call | tf_op jit(solution)/shard_map/finish/pallas_call | solution.py:363
  (3 shorter events, 0.0 us)
Async XLA Ops:
  0.6 1.4 %copy-start = (f32[8,160]{1,0:T(8,128)S(1)}, f32[8,160]{1,0:T(8,128)}, u32[]{:S(2)}) copy-start(f32[8,160]{1,0:T(8,128)} %param.5) | copy-start | bytes 15364
  2.0 0.7 copy-start.1

commit v4 on v3

--- a/solution.py
+++ b/solution.py
@@ -10,6 +10,7 @@
 HIGHEST = lax.Precision.HIGHEST
 FAR = 5000.0
 VMEM = pl.BlockSpec(memory_space=pltpu.VMEM)
+SMEM = pl.BlockSpec(memory_space=pltpu.SMEM)
 
 
 def dot(a, b, dims, precision=HIGHEST):
@@ -38,7 +39,7 @@
 
 
 def tile_kernel(
-    rows, cols, info, tests, out, srcs, tgts, bank, left,
+    rows, cols, points, tests, rank, boundary, scales, out, info, srcs, tgts, bank, left,
     s_tgt, r_tgt, s_along, r_along, s_info, r_info, s_over, r_over, s_mate, r_mate,
 ):
     row, col = lax.axis_index("row"), lax.axis_index("col")
@@ -58,8 +59,27 @@
     each(1, cols, lambda k: pl.semaphore_signal(barrier, 1, device_id=(row, (col + k) % cols), device_id_type=mesh))
     each(1, lines, lambda k: pl.semaphore_signal(barrier, 1, device_id=(at(k), col), device_id_type=mesh))
     pl.semaphore_signal(barrier, 1, device_id=(mate, col), device_id_type=mesh)
-    srcs[row] = info[...]
-    tgts[col] = info[...]
+    sq = points.shape[0]
+    spot = lax.broadcasted_iota(jnp.int32, points.shape, 0)
+    scale = jnp.ones(points.shape, jnp.float32)
+    for i in range(sq):
+        scale = jnp.where(spot == i, scales[i], scale)
+    scaled = points[...] / scale
+    side = jnp.where(rank[...] >= boundary[0], 1.0, 0.0)
+    own = jnp.concatenate(
+        [
+            scaled,
+            -0.5 * jnp.sum(scaled * scaled, axis=0, keepdims=True),
+            jnp.ones_like(side),
+            side,
+            1.0 - side,
+            jnp.zeros((info.shape[0] - sq - 4, local), jnp.float32),
+        ],
+        axis=0,
+    )
+    info[...] = own
+    srcs[row] = own
+    tgts[col] = own
     bank[row] = tests[...]
     pl.semaphore_wait(barrier, cols + lines - 1)
 
@@ -101,7 +121,6 @@
     go(first())
     each(1, lines, lambda k: go(along(k)))
     each(1, cols, lambda k: tgt(k).wait())
-    sq = 8
     for place in range(cols):
         block = tgts[2 * (place % (cols // 2)) + place // (cols // 2)]
         half, one = block[sq : sq + 1], block[sq + 1 : sq + 2]
@@ -139,17 +158,18 @@
     each(1, lines, lambda k: leave(along(k) + over(k)))
 
 
-def tiles(info, tests, rows, cols):
-    depth, local = info.shape
+def tiles(points, tests, rank, boundary, scales, rows, cols):
+    depth, local = 8 * ((points.shape[0] + 11) // 8), points.shape[1]
     ranks = tests.shape[1]
     lines = rows // 2
     dma = pltpu.SemaphoreType.DMA
     return pl.pallas_call(
         functools.partial(tile_kernel, rows, cols),
         out_shape=jax.ShapeDtypeStruct((cols * local, ranks), jnp.float32),
-        in_specs=[VMEM, VMEM],
+        in_specs=[VMEM, VMEM, VMEM, SMEM, SMEM],
         out_specs=VMEM,
         scratch_shapes=[
+            pltpu.VMEM((depth, local), jnp.float32),
             pltpu.VMEM((rows, depth, local), jnp.float32),
             pltpu.VMEM((cols, depth, local), jnp.float32),
             pltpu.VMEM((rows, local, ranks), tests.dtype),
@@ -160,7 +180,7 @@
         ],
         compiler_params=pltpu.CompilerParams(collective_id=0, has_side_effects=True),
         name="tiles",
-    )(info, tests)
+    )(points, tests, rank[None], boundary, scales)
 
 
 def reduce_kernel(
@@ -374,12 +394,7 @@
 
 
 def body(rows, cols, points, sketch, rank, boundary, scales):
-    scaled = points / scales[:, None]
-    side = (rank >= boundary[0]).astype(jnp.float32)[None]
-    down = -0.5 * jnp.sum(scaled * scaled, axis=0, keepdims=True)
-    fill = jnp.zeros((4, points.shape[1]), jnp.float32)
-    info = jnp.concatenate([scaled, down, jnp.ones_like(side), side, 1.0 - side, fill], axis=0)
-    sample, gram = reduce(tiles(info, sketch, rows, cols), rows, cols)
+    sample, gram = reduce(tiles(points, sketch, rank, boundary, scales, rows, cols), rows, cols)
     return finish(gram, sample, rows * cols * points.shape[1])
 
 

time: 69.1 us -> 66.4 us (0.961)
  local copies, waits for them, and re-layouts: 1.88 us -> 0 us
  other arithmetic: 0.77 us -> 0 us
    concatenate x1 -> x0, local copies, waits for them, and re-layouts: 1.22 us -> none  [body(): jnp.concatenate([scaled, down, jnp.ones_like(side), side, 1.0 - side, fil...]
where the time goes in v4:
time: 66.4 us; the launch traced here: 66.2 us
  Pallas kernels  64.9 us (98%)
  between operations  1.29 us (2%)
    pallas_call x1, Pallas kernels, reduce(): pl.pallas_call(functools.partial(reduce_kernel, rows, cols), out_shape=(j...  27.9 us
    pallas_call x1, Pallas kernels, tiles(): pl.pallas_call(functools.partial(tile_kernel, rows, cols), out_shape=jax....  23.3 us
    pallas_call x1, Pallas kernels, finish(): pl.pallas_call(functools.partial(finish_kernel, 1.0 / everyone), out_shap...  13.8 us

profile of v4, /device:TPU:0, one launch (start us, length us, event | category | flops | bytes accessed | tf_op | source)
XLA Modules:
  0.0 66.2 jit_solution(3639975585981655172)
XLA Ops:
  1.3 23.3 %tiles.1 = f32[640,256]{1,0:T(8,128)} custom-call(f32[8,160]{1,0:T(8,128)} %points.1, bf16[160,256]{1,0:T(8,128)(2,1)} %tests.1, s32[1,160]{1,0:T(1,128)} %bitcast.5, s32[1]{0:T(128)S(6)} %copy.7.boundary, f32[8]{0:T(128)} %scales.1), custom_call_target="tpu_custom_call" | custom-call | tf_op jit(solution)/shard_map/tiles/pallas_call | solution.py:166
  24.6 27.9 %reduce.1 = (f32[160,256]{1,0:T(8,128)}, f32[2,16,8,256]{3,2,1,0:T(8,128)}) custom-call(f32[2,2,160,256]{3,2,1,0:T(8,128)} %bitcast.3), custom_call_target="tpu_custom_call" | custom-call | tf_op jit(solution)/shard_map/reduce/pallas_call | solution.py:276
  52.4 13.8 %finish.1 = (f32[160,256]{1,0:T(8,128)}, f32[256,256]{1,0:T(8,128)}) custom-call(f32[256,256]{1,0:T(8,128)} %bitcast.4, f32[160,256]{1,0:T(8,128)} %get-tuple-element.5.sample), custom_call_target="tpu_custom_call" | custom-call | tf_op jit(solution)/shard_map/finish/pallas_call | solution.py:383
